TPU v7x, 256 devices: a whole 4x4x8 slice. The times are simulated.
256 devices in a mesh: grp: 4 (over y), shard: 64 (over z, x, core).
Axes of the slice: x: 4, y: 4, z: 8, core: 2. Of those that a mesh axis runs over, the one named last changes fastest.
Arguments:
- query_rows: bfloat16 [65536, 1024], P(('grp', 'shard')), may hold values from -6 to 6
- key_rows: bfloat16 [65536, 1024], P(('grp', 'shard')), may hold values from -6 to 6
- value_rows: bfloat16 [65536, 1024], P(('grp', 'shard')), may hold values from -6 to 6
- grad_out: bfloat16 [65536, 1024], P(('grp', 'shard')), may hold values from -6 to 6
Outputs:
- attended: bfloat16 [65536, 1024], P(('grp', 'shard'))
- grad_query: bfloat16 [65536, 1024], P(('grp', 'shard'))
- grad_key: bfloat16 [65536, 1024], P(('grp', 'shard'))
- grad_value: bfloat16 [65536, 1024], P(('grp', 'shard'))
All inputs are finite; a program needn't handle non-finite values.
Results may differ from a plain program's by a relative error of at most 0.012.
Values may be sent and summed in bfloat16 or wider, within the bound.
A program may use at most 256 MiB of HBM per device.

v0:
```python
import jax
import jax.numpy as jnp
from jax import lax
from jax.sharding import PartitionSpec as P

HD = 128


def entering(array, axis, join, neutral, backward):
    count = lax.axis_size(axis)
    place = lax.axis_index(axis)
    ahead = count - 1 - place if backward else place
    gathered = lax.all_gather(array.astype(jnp.bfloat16), axis)
    state = jnp.zeros_like(array) + jnp.asarray(neutral, array.dtype)

    def one(step, state):
        source = count - 1 - step if backward else step
        return join(state, lax.dynamic_index_in_dim(gathered, source, 0, False).astype(array.dtype))

    return lax.fori_loop(0, ahead, one, state)


def add_states(earlier, later_part):
    return earlier + later_part


def prefix_states(local_state, backward):
    empty_state = jnp.zeros_like(local_state)
    inside = entering(local_state, "shard", add_states, empty_state, backward)
    group_sum = lax.psum(local_state, "shard")
    outside = entering(group_sum, "grp", add_states, empty_state, backward)
    return inside + outside


def body(query_rows, key_rows, value_rows, grad_out):
    row_count = query_rows.shape[0]
    head_size = HD
    head_count = query_rows.shape[1] // head_size
    query_heads = query_rows.reshape(row_count, head_count, head_size)
    key_heads = key_rows.reshape(row_count, head_count, head_size)
    value_heads = value_rows.reshape(row_count, head_count, head_size)
    rows_at = lax.broadcasted_iota(jnp.int32, (row_count, row_count), 0)
    cols_at = lax.broadcasted_iota(jnp.int32, (row_count, row_count), 1)
    causal = (rows_at >= cols_at)[None]
    block_state = jnp.einsum(
        "thd,the->hde", key_heads, value_heads, preferred_element_type=jnp.float32
    )
    earlier = prefix_states(block_state, False)
    scores = jnp.einsum("thd,shd->hts", query_heads, key_heads, preferred_element_type=jnp.float32)
    local_scores = jnp.where(causal, scores, 0.0).astype(jnp.bfloat16)
    local_mixed = jnp.einsum(
        "hts,she->the", local_scores, value_heads, preferred_element_type=jnp.float32
    )
    earlier_rounded = earlier.astype(jnp.bfloat16)
    mixed_rows = local_mixed + jnp.einsum(
        "thd,hde->the", query_heads, earlier_rounded, preferred_element_type=jnp.float32
    )
    inv_rms = lax.rsqrt(jnp.mean(mixed_rows * mixed_rows, axis=-1, keepdims=True) + 1.0)
    normed = mixed_rows * inv_rms
    attended = normed.astype(jnp.bfloat16).reshape(row_count, head_count * head_size)
    grad_heads = grad_out.reshape(row_count, head_count, head_size).astype(jnp.float32)
    grad_mixed = (
        (grad_heads - normed * jnp.mean(grad_heads * normed, axis=-1, keepdims=True)) * inv_rms
    ).astype(jnp.bfloat16)
    block_reverse = jnp.einsum(
        "thd,the->hde", query_heads, grad_mixed, preferred_element_type=jnp.float32
    )
    later_sum = prefix_states(block_reverse, True)
    grad_raw = jnp.einsum(
        "the,she->hts", grad_mixed, value_heads, preferred_element_type=jnp.float32
    )
    grad_scores = jnp.where(causal, grad_raw, 0.0).astype(jnp.bfloat16)
    grad_query = jnp.einsum(
        "hts,shd->thd", grad_scores, key_heads, preferred_element_type=jnp.float32
    )
    grad_query = grad_query + jnp.einsum(
        "the,hde->thd", grad_mixed, earlier_rounded, preferred_element_type=jnp.float32
    )
    key_local = jnp.einsum(
        "hts,thd->shd", grad_scores, query_heads, preferred_element_type=jnp.float32
    )
    value_local = jnp.einsum(
        "hts,the->she", local_scores, grad_mixed, preferred_element_type=jnp.float32
    )
    later_rounded = later_sum.astype(jnp.bfloat16)
    grad_key = key_local + jnp.einsum(
        "she,hde->shd", value_heads, later_rounded, preferred_element_type=jnp.float32
    )
    grad_value = value_local + jnp.einsum(
        "shd,hde->she", key_heads, later_rounded, preferred_element_type=jnp.float32
    )
    flat_width = head_count * head_size
    return (
        attended,
        grad_query.astype(jnp.bfloat16).reshape(row_count, flat_width),
        grad_key.astype(jnp.bfloat16).reshape(row_count, flat_width),
        grad_value.astype(jnp.bfloat16).reshape(row_count, flat_width),
    )


def solution(mesh):
    in_specs = (
        P(("grp", "shard"), None),
        P(("grp", "shard"), None),
        P(("grp", "shard"), None),
        P(("grp", "shard"), None),
    )
    out_specs = (
        P(("grp", "shard"), None),
        P(("grp", "shard"), None),
        P(("grp", "shard"), None),
        P(("grp", "shard"), None),
    )
    return jax.shard_map(body, mesh=mesh, in_specs=in_specs, out_specs=out_specs, check_vma=False)
```

profile of v0, /device:TPU:1, one launch (start us, length us, event | category | flops | bytes accessed | tf_op | source)
XLA Modules:
  0.0 917.8 jit_solution(16972495328482349829)
XLA Ops:
  7.2 1.2 copy.61
  9.8 252.9 %all-reduce.2 = bf16[8,128,128]{2,1,0:T(8,128)(2,1)} all-reduce(f32[8,128,128]{2,1,0:T(8,128)S(1)} %get-tuple-element.217), channel_id=1, replica_groups=mesh['grp'=4,'shard'=64] {'shard'}, use_global_device_ids=true, to_apply=%region_2.3 | all-reduce | flops 131072 | bytes 786432 | tf_op jit(solution)/shard_map/psum | solution.py:30
  263.5 1.2 copy.38
  266.3 1.5 convolution_bitcast_fusion.5
  267.7 19.5 %all-gather.11.cloned.1.call-done = bf16[32,128,128]{2,1,0:T(8,128)(2,1)} async-done(((bf16[8,128,128]{2,1,0:T(8,128)(2,1)}), bf16[32,128,128]{2,1,0:T(8,128)(2,1)}) %all-gather.11.cloned.1.call-update) | async-done | bytes 1048592 | tf_op jit(solution)/shard_map/all_gather | solution.py:13
  287.3 105.4 %all-gather.9.cloned.1.call-done = bf16[512,128,128]{2,1,0:T(8,128)(2,1)} async-done(((bf16[8,128,128]{2,1,0:T(8,128)(2,1)}), bf16[512,128,128]{2,1,0:T(8,128)(2,1)}) %all-gather.9.cloned.1.call-update) | async-done | bytes 16777232 | tf_op jit(solution)/shard_map/all_gather | solution.py:13
  392.7 1.1 while.44
  393.9 1.6 multiply_reduce_fusion.1
  397.0 313.1 %all-reduce.3 = bf16[8,128,128]{1,2,0:T(8,128)(2,1)S(1)} all-reduce(f32[8,128,128]{1,2,0:T(8,128)S(1)} %get-tuple-element.221), channel_id=1, replica_groups=mesh['grp'=4,'shard'=64] {'shard'}, use_global_device_ids=true, to_apply=%region_9.10 | all-reduce | flops 131072 | bytes 786432 | tf_op jit(solution)/shard_map/psum | solution.py:30
  712.9 1.1 fusion.3
  714.0 2.0 copy.51
  717.0 1.3 fusion.29
  718.7 15.7 %all-gather.15.cloned.1.call-done = bf16[32,128,128]{2,1,0:T(8,128)(2,1)} async-done(((bf16[8,128,128]{2,1,0:T(8,128)(2,1)}), bf16[32,128,128]{2,1,0:T(8,128)(2,1)}) %all-gather.15.cloned.1.call-update) | async-done | bytes 1048592 | tf_op jit(solution)/shard_map/all_gather | solution.py:13
  734.4 3.3 while.47
  734.4 1.1 convert_add_fusion.11
  735.5 1.1 convert_add_fusion.11
  736.6 1.1 convert_add_fusion.11
  737.7 101.4 %all-gather.13.cloned.1.call-done = bf16[512,128,128]{2,1,0:T(8,128)(2,1)} async-done(((bf16[8,128,128]{2,1,0:T(8,128)(2,1)}), bf16[512,128,128]{2,1,0:T(8,128)(2,1)}) %all-gather.13.cloned.1.call-update) | async-done | bytes 16777232 | tf_op jit(solution)/shard_map/all_gather | solution.py:13
  839.1 68.0 %while.46 = (s32[]{:T(128)}, f32[8,128,128]{2,1,0:T(8,128)S(1)}, s32[]{:T(128)}, bf16[64,8,128,128]{3,2,1,0:T(8,128)(2,1)}, s32[]{:T(128)}, /*index=5*/s32[]{:T(128)}, s32[]{:T(128)}, s32[]{:T(128)}) while((s32[]{:T(128)}, f32[8,128,128]{2,1,0:T(8,128)S(1)}, s32[]{:T(128)}, bf16[64,8,128,128]{3,2,1,0:T(8,128)(2,1)}, s32[]{:T(128)}, ...), condition=%wide.region_8.9_spmd, body=%wide.region_7.8_spmd.sunk | while | flops 262150 | bytes 1310855 | solution.py:20
  840.2 1.1 convert_add_fusion.10
  841.3 1.1 convert_add_fusion.10
  842.4 1.1 convert_add_fusion.10
  843.5 1.1 convert_add_fusion.10
  844.6 1.1 convert_add_fusion.10
  845.7 1.1 convert_add_fusion.10
  846.8 1.1 convert_add_fusion.10
  851.2 1.1 convert_add_fusion.10
  852.3 1.1 convert_add_fusion.10
  853.4 1.1 convert_add_fusion.10
  854.5 1.1 convert_add_fusion.10
  855.6 1.1 convert_add_fusion.10
  907.2 1.7 fusion.5
  (106 shorter events, 66.3 us)
Async XLA Ops:
  7.2 257.7 %copy-start = (bf16[256,1024]{1,0:T(8,128)(2,1)S(1)}, bf16[256,1024]{1,0:T(8,128)(2,1)}, u32[]{:S(2)}) copy-start(bf16[256,1024]{1,0:T(8,128)(2,1)} %param.12) | copy-start | bytes 1572868
  7.2 1.6 copy-start.3
  7.2 280.0 %all-gather.11.cloned.1.call-start = ((), (), s32[]{:S(2)}) async-start(), calls=%async_computation.1 | async-start | bytes 1310720 | tf_op jit(solution)/shard_map/all_gather | solution.py:13
  8.8 256.0 %copy-start.1 = (bf16[256,8,128]{0,2,1:T(8,128)(2,1)}, bf16[256,8,128]{0,2,1:T(8,128)(2,1)S(1)}, u32[]{:S(2)}) copy-start(bf16[256,8,128]{0,2,1:T(8,128)(2,1)S(1)} %copy.34) | copy-start | bytes 1572868
  8.8 256.0 %copy-start.9 = (bf16[256,1024]{1,0:T(8,128)(2,1)S(1)}, bf16[256,1024]{1,0:T(8,128)(2,1)}, u32[]{:S(2)}) copy-start(bf16[256,1024]{1,0:T(8,128)(2,1)} %param.13) | copy-start | bytes 1572868
  262.7 129.9 %all-gather.9.cloned.1.call-start = ((), (), s32[]{:S(2)}) async-start(), calls=%async_computation | async-start | bytes 17039360 | tf_op jit(solution)/shard_map/all_gather | solution.py:13
  263.5 470.9 %all-gather.15.cloned.1.call-start = ((), (), s32[]{:S(2)}) async-start(), calls=%async_computation.3 | async-start | bytes 1310720 | tf_op jit(solution)/shard_map/all_gather | solution.py:13
  265.3 1.0 copy-start.5
  396.7 315.2 %copy-start.4 = (bf16[256,1024]{1,0:T(8,128)(2,1)S(1)}, bf16[256,1024]{1,0:T(8,128)(2,1)}, u32[]{:S(2)}) copy-start(bf16[256,1024]{1,0:T(8,128)(2,1)} %param.14) | copy-start | bytes 1572868
  710.0 2.3 copy-start.2
  710.9 128.1 %all-gather.13.cloned.1.call-start = ((), (), s32[]{:S(2)}) async-start(), calls=%async_computation.2 | async-start | bytes 17039360 | tf_op jit(solution)/shard_map/all_gather | solution.py:13
  712.4 1.6 copy-start.7
  712.9 3.1 copy-start.10
  712.9 4.1 copy-start.6
  717.0 1.3 copy-start.8
Sparse Core Ops, SparseCore 0:
  262.9 24.3 all-gather.10
  290.6 102.0 all-gather.8
  711.0 23.2 all-gather.14
  737.0 102.0 all-gather.12
where the time goes:
time: 920 us; the launch traced here: 918 us
  blocking collectives  566 us (62%)
  waiting for transfers between devices  243 us (26%)
  other arithmetic  71.9 us (8%)
  between operations  14 us (2%)
  local copies, waits for them, and re-layouts  10.7 us (1%)
  matrix products  10.5 us (1%)
    psum x2, blocking collectives, prefix_states(): group_sum = lax.psum(local_state, 'shard')  566 us
    all_gather x4, waiting for transfers between devices, entering(): gathered = lax.all_gather(array.astype(jnp.bfloat16), axis)  242 us
    add x66, other arithmetic, add_states(): return earlier + later_part  70.6 us
  transfers between devices with their start and end apart: 4, of which 4 were waited for; matrix products, arithmetic and copies ran while one was open for 2% of the time, Pallas kernels for 0%

commit v1 on v0

--- a/solution.py
+++ b/solution.py
@@ -27,7 +27,7 @@
 def prefix_states(local_state, backward):
     empty_state = jnp.zeros_like(local_state)
     inside = entering(local_state, "shard", add_states, empty_state, backward)
-    group_sum = lax.psum(local_state, "shard")
+    group_sum = jnp.sum(lax.all_gather(local_state, axis_name="shard"), axis=0)
     outside = entering(group_sum, "grp", add_states, empty_state, backward)
     return inside + outside
 

time: 920 us -> 653 us (0.71)
  blocking collectives: 566 us -> 0 us
  waiting for transfers between devices: 243 us -> 513 us
  other arithmetic: 71.9 us -> 96.4 us
    psum x2 -> x0, blocking collectives: 566 us -> none  [prefix_states(): group_sum = lax.psum(local_state, 'shard')]
    all_gather x0 -> x2, waiting for transfers between devices: none -> 322 us  [prefix_states(): group_sum = jnp.sum(lax.all_gather(local_state, axis_name='shard'), axis=0)]
    all_gather x4, waiting for transfers between devices: 242 us -> 190 us  [entering(): gathered = lax.all_gather(array.astype(jnp.bfloat16), axis)]
    reduce_sum x0 -> x2, other arithmetic: none -> 24.4 us  [prefix_states(): group_sum = jnp.sum(lax.all_gather(local_state, axis_name='shard'), axis=0)]
  transfers between devices with their start and end apart: 4 -> 6, of which waited for: 4 -> 5; matrix products, arithmetic and copies ran while one was open for 2% -> 16% of each run, Pallas kernels for 0% -> 0%
where the time goes in v1:
time: 653 us; the launch traced here: 651 us
  waiting for transfers between devices  513 us (79%)
  other arithmetic  96.4 us (15%)
  between operations  14.4 us (2%)
  matrix products  13.2 us (2%)
  local copies, waits for them, and re-layouts  12.3 us (2%)
    all_gather x2, waiting for transfers between devices, prefix_states(): group_sum = jnp.sum(lax.all_gather(local_state, axis_name='shard'), axis=0)  322 us
    all_gather x4, waiting for transfers between devices, entering(): gathered = lax.all_gather(array.astype(jnp.bfloat16), axis)  190 us
    add x66, other arithmetic, add_states(): return earlier + later_part  70.6 us
    reduce_sum x2, other arithmetic, prefix_states(): group_sum = jnp.sum(lax.all_gather(local_state, axis_name='shard'), axis=0)  24.4 us
  transfers between devices with their start and end apart: 6, of which 5 were waited for; matrix products, arithmetic and copies ran while one was open for 16% of the time, Pallas kernels for 0%

profile of v1, /device:TPU:1, one launch (start us, length us, event | category | flops | bytes accessed | tf_op | source)
XLA Modules:
  0.0 650.9 jit_solution(13207112905633814764)
XLA Ops:
  7.2 1.2 copy.63
  8.7 2.2 fusion.27
  11.8 1.2 copy.37
  13.1 144.1 %all-gather.15.cloned.1.call-done = f32[512,128,128]{2,1,0:T(8,128)} async-done(((f32[8,128,128]{2,1,0:T(8,128)}), f32[512,128,128]{2,1,0:T(8,128)}) %all-gather.15.cloned.1.call-update) | async-done | bytes 33554448 | tf_op jit(solution)/shard_map/all_gather | solution.py:30
  157.1 12.6 %reduce_sum.36 = bf16[8,128,128]{2,1,0:T(8,128)(2,1)} reduce(f32[64,8,128,128]{3,2,1,0:T(8,128)} %bitcast.138, f32[]{:T(128)} %constant.79.clone.1), dimensions={0}, to_apply=%region_2.3 | reduce | flops 8257536 | bytes 33816580 | tf_op jit(solution)/shard_map/reduce_sum | solution.py:30
  171.3 1.5 convolution_bitcast_fusion.5
  172.8 83.9 %all-gather.13.cloned.1.call-done = bf16[512,128,128]{2,1,0:T(8,128)(2,1)} async-done(((bf16[8,128,128]{2,1,0:T(8,128)(2,1)}), bf16[512,128,128]{2,1,0:T(8,128)(2,1)}) %all-gather.13.cloned.1.call-update) | async-done | bytes 16777232 | tf_op jit(solution)/shard_map/all_gather | solution.py:13
  256.8 1.1 while.44
  256.8 1.1 convert_add_fusion.8
  257.9 22.5 %all-gather.17.cloned.1.call-done = bf16[32,128,128]{2,1,0:T(8,128)(2,1)} async-done(((bf16[8,128,128]{2,1,0:T(8,128)(2,1)}), bf16[32,128,128]{2,1,0:T(8,128)(2,1)}) %all-gather.17.cloned.1.call-update) | async-done | bytes 1048592 | tf_op jit(solution)/shard_map/all_gather | solution.py:13
  280.5 1.6 multiply_reduce_fusion.1
  285.6 1.5 select_convert_fusion
  289.4 2.0 copy.51
  291.4 178.2 %all-gather.21.cloned.1.call-done = f32[512,128,128]{2,1,0:T(8,128)} async-done(((f32[8,128,128]{2,1,0:T(8,128)}), f32[512,128,128]{2,1,0:T(8,128)}) %all-gather.21.cloned.1.call-update) | async-done | bytes 33554448 | tf_op jit(solution)/shard_map/all_gather | solution.py:30
  469.6 11.8 %reduce_sum.39 = bf16[8,128,128]{2,1,0:T(8,128)(2,1)S(1)} reduce(f32[64,8,128,128]{3,2,1,0:T(8,128)} %bitcast.137, f32[]{:T(128)} %constant.79.clone.1), dimensions={0}, to_apply=%region_9.10 | reduce | flops 8257536 | bytes 33816580 | tf_op jit(solution)/shard_map/reduce_sum | solution.py:30
  482.5 1.3 fusion.29
  483.8 1.6 convolution_bitcast_fusion.3
  485.3 83.1 %all-gather.19.cloned.1.call-done = bf16[512,128,128]{2,1,0:T(8,128)(2,1)} async-done(((bf16[8,128,128]{2,1,0:T(8,128)(2,1)}), bf16[512,128,128]{2,1,0:T(8,128)(2,1)}) %all-gather.19.cloned.1.call-update) | async-done | bytes 16777232 | tf_op jit(solution)/shard_map/all_gather | solution.py:13
  568.5 68.0 %while.46 = (s32[]{:T(128)}, f32[8,128,128]{2,1,0:T(8,128)S(1)}, s32[]{:T(128)}, bf16[64,8,128,128]{3,2,1,0:T(8,128)(2,1)}, s32[]{:T(128)}, /*index=5*/s32[]{:T(128)}, s32[]{:T(128)}, s32[]{:T(128)}) while((s32[]{:T(128)}, f32[8,128,128]{2,1,0:T(8,128)S(1)}, s32[]{:T(128)}, bf16[64,8,128,128]{3,2,1,0:T(8,128)(2,1)}, s32[]{:T(128)}, ...), condition=%wide.region_8.9_spmd, body=%wide.region_7.8_spmd.sunk | while | flops 262150 | bytes 1310855 | solution.py:20
  571.8 1.1 convert_add_fusion.10
  572.9 1.1 convert_add_fusion.10
  574.0 1.1 convert_add_fusion.10
  575.1 1.1 convert_add_fusion.10
  576.2 1.1 convert_add_fusion.10
  577.3 1.1 convert_add_fusion.10
  578.4 1.1 convert_add_fusion.10
  583.9 1.1 convert_add_fusion.10
  585.0 1.1 convert_add_fusion.10
  587.2 1.1 convert_add_fusion.10
  588.3 1.1 convert_add_fusion.10
  636.6 3.3 while.47
  640.0 1.7 fusion.5
  (106 shorter events, 69.8 us)
Async XLA Ops:
  7.2 162.7 %copy-start = (bf16[256,1024]{1,0:T(8,128)(2,1)S(1)}, bf16[256,1024]{1,0:T(8,128)(2,1)}, u32[]{:S(2)}) copy-start(bf16[256,1024]{1,0:T(8,128)(2,1)} %param.12) | copy-start | bytes 1572868
  7.2 150.0 %all-gather.15.cloned.1.call-start = ((), (), s32[]{:S(2)}) async-start(), calls=%async_computation.1 | async-start | bytes 34078720 | tf_op jit(solution)/shard_map/all_gather | solution.py:30
  11.0 245.7 %all-gather.13.cloned.1.call-start = ((), (), s32[]{:S(2)}) async-start(), calls=%async_computation | async-start | bytes 17039360 | tf_op jit(solution)/shard_map/all_gather | solution.py:13
  11.7 268.6 %all-gather.17.cloned.1.call-start = ((), (), s32[]{:S(2)}) async-start(), calls=%async_computation.2 | async-start | bytes 1310720 | tf_op jit(solution)/shard_map/all_gather | solution.py:13
  157.1 12.7 %copy-start.6 = (bf16[256,1024]{1,0:T(8,128)(2,1)S(1)}, bf16[256,1024]{1,0:T(8,128)(2,1)}, u32[]{:S(2)}) copy-start(bf16[256,1024]{1,0:T(8,128)(2,1)} %param.13) | copy-start | bytes 1572868
  157.1 14.2 %copy-start.1 = (bf16[256,1024]{1,0:T(8,128)(2,1)S(1)}, bf16[256,1024]{1,0:T(8,128)(2,1)}, u32[]{:S(2)}) copy-start(bf16[256,1024]{1,0:T(8,128)(2,1)} %param.14) | copy-start | bytes 1572868
  169.8 299.8 %all-gather.21.cloned.1.call-start = ((), (), s32[]{:S(2)}) async-start(), calls=%async_computation.4 | async-start | bytes 34078720 | tf_op jit(solution)/shard_map/all_gather | solution.py:30
  170.3 1.0 copy-start.3
  284.6 283.8 %all-gather.19.cloned.1.call-start = ((), (), s32[]{:S(2)}) async-start(), calls=%async_computation.3 | async-start | bytes 17039360 | tf_op jit(solution)/shard_map/all_gather | solution.py:13
  285.5 351.0 %all-gather.23.cloned.1.call-start = ((), (), s32[]{:S(2)}) async-start(), calls=%async_computation.5 | async-start | bytes 1310720 | tf_op jit(solution)/shard_map/all_gather | solution.py:13
  287.1 1.0 copy-start.5
  469.6 12.9 %copy-start.4 = (bf16[8,256,256]{2,1,0:T(8,128)(2,1)S(1)}, bf16[8,256,256]{2,1,0:T(8,128)(2,1)}, u32[]{:S(2)}) copy-start(bf16[8,256,256]{2,1,0:T(8,128)(2,1)} %copy-done.3) | copy-start | bytes 3145732
  481.4 161.3 %copy-start.2 = (bf16[256,1024]{1,0:T(8,128)(2,1)S(1)}, bf16[256,1024]{1,0:T(8,128)(2,1)}, u32[]{:S(2)}) copy-start(bf16[256,1024]{1,0:T(8,128)(2,1)} %param.14) | copy-start | bytes 1572868
Sparse Core Ops, SparseCore 0:
  11.3 145.7 all-gather.14
  160.5 96.1 all-gather.12
  259.1 21.2 all-gather.16
  284.7 184.8 all-gather.20
  472.2 96.1 all-gather.18
  570.7 21.2 all-gather.22
